TPU v7x, 32 devices: a whole 2x2x4 slice. The times are simulated.
32 devices in a mesh: dp: 8 (over z, y), row: 2 (over x), col: 2 (over core).
Axes of the slice: x: 2, y: 2, z: 4, core: 2. Of those that a mesh axis runs over, the one named last changes fastest.
Arguments:
- tokens: bfloat16 [12288, 1024], P('dp', 'row'), may hold values from -6 to 6
- gain_attn: float32 [1024], replicated, may hold values from 0.5 to 1.5
- w_qkv: float32 [1024, 16, 192], P('row', 'col'), may hold values from -0.1875 to 0.1875
- w_out: float32 [1024, 1024], P('col', 'row'), may hold values from -3 to 3
- gain_mlp: float32 [1024], replicated, may hold values from 0.5 to 1.5
- w_in: float32 [1024, 2, 2624], P('row', None, 'col'), may hold values from -0.1875 to 0.1875
- w_down: float32 [2624, 1024], P('col', 'row'), may hold values from -0.125 to 0.125
- cotangent: bfloat16 [12288, 1024], P('dp', 'row'), may hold values from -6 to 6
- seq_lengths: int32 [16], replicated, may hold values from 256 to 1024, as said below
- seq_offsets: int32 [16], replicated, may hold values from 0 to 11264, as said below
- deal: int32 [16], replicated, may hold values from 0 to 15, as said below
Outputs:
- layer_out: bfloat16 [12288, 1024], P('dp', 'row')
- tokens_grad: bfloat16 [12288, 1024], P('dp', 'row')
- gain_attn_grad: float32 [1024], P(('dp', 'row'))
- w_qkv_grad: float32 [1024, 16, 192], P(('dp', 'row'), 'col')
- w_out_grad: float32 [1024, 1024], P('col', ('dp', 'row'))
- gain_mlp_grad: float32 [1024], P(('dp', 'row'))
- w_in_grad: float32 [1024, 2, 2624], P(('dp', 'row'), None, 'col')
- w_down_grad: float32 [2624, 1024], P('col', ('dp', 'row'))
Inputs may be any that keep to these rules, and one draw needn't show every extreme that they name: `seq_lengths`: each group holds one sequence of 1024 tokens, its others have at most half of 1024, and some group fills all 1536 slots. Sequence 16 - 1 has 1024 tokens. Sequences 0 to 14 lie end to end in index order from place 0: seq_offsets[s] is the sum of the lengths of sequences 0 to s - 1. Sequence 16 - 1 ends at the last token place; places between belong to no sequence. `deal`: A permutation of the 16 sequences.
All inputs are finite; a program needn't handle non-finite values.
Results may differ from a plain program's by a relative error of at most 0.017.
Values may be sent and summed in bfloat16 or wider, within the bound.
No kernel may reach another device: no remote copies, remote signals or barrier semaphores. Data moves between devices by JAX's collectives and lax.ppermute only.
A program may use at most 192 MiB of HBM per device.

v0:
```python
import math
import jax
import jax.numpy as jnp
from jax import lax
from jax.sharding import PartitionSpec as P

SEQ_GRP = 2
CAP = 1536
epsilon = 1e-05
rope_base = 160000.0


def slot_table(seq_lengths, seq_offsets, deal, group_index):
    members = lax.dynamic_slice_in_dim(deal, group_index * SEQ_GRP, SEQ_GRP)
    every = jnp.arange(deal.shape[0], dtype=jnp.int32)
    matches = every[None, :] == members[:, None]
    member_lengths = jnp.sum(jnp.where(matches, seq_lengths[None, :], 0), axis=1)
    member_offsets = jnp.sum(jnp.where(matches, seq_offsets[None, :], 0), axis=1)
    member_starts = jnp.cumsum(member_lengths) - member_lengths
    slots = jnp.arange(CAP, dtype=jnp.int32)
    inside = (slots[:, None] >= member_starts[None, :]) & (
        slots[:, None] < (member_starts + member_lengths)[None, :]
    )
    live = jnp.any(inside, axis=1)
    places = slots - jnp.sum(jnp.where(inside, member_starts[None, :], 0), axis=1)
    segment = jnp.sum(
        jnp.where(inside, jnp.arange(SEQ_GRP, dtype=jnp.int32)[None, :], 0), axis=1
    ) + jnp.where(live, 0, SEQ_GRP)
    source = jnp.where(
        live, jnp.sum(jnp.where(inside, member_offsets[None, :], 0), axis=1) + places, -1
    )
    return (source, places, segment)


def home_slots(seq_lengths, seq_offsets, deal, group_index, block_length):
    every = jnp.arange(deal.shape[0], dtype=jnp.int32)
    dealt = deal[None, :] == every[:, None]
    place_of = jnp.sum(jnp.where(dealt, every[None, :], 0), axis=1)
    dealt_lengths = jnp.sum(jnp.where(dealt, seq_lengths[:, None], 0), axis=0)
    grouped = dealt_lengths.reshape(-1, SEQ_GRP)
    place_starts = (jnp.cumsum(grouped, axis=1) - grouped).reshape(-1)
    slot_starts = jnp.sum(jnp.where(dealt, place_starts[None, :], 0), axis=1)
    homes = place_of // SEQ_GRP * CAP + slot_starts - seq_offsets
    given = group_index * block_length + jnp.arange(block_length, dtype=jnp.int32)
    inside = (given[:, None] >= seq_offsets[None, :]) & (
        given[:, None] < (seq_offsets + seq_lengths)[None, :]
    )
    target = jnp.where(
        jnp.any(inside, axis=1), jnp.sum(jnp.where(inside, homes[None, :], 0), axis=1) + given, -1
    )
    return target


def take_rows(kept, incoming, relative):
    row_count = incoming[0].shape[0]
    usable = ((relative >= 0) & (relative < row_count))[:, None]
    picked = jnp.clip(relative, 0, row_count - 1)
    return tuple(
        (
            jnp.where(usable, jnp.take(arriving, picked, axis=0), holding)
            for holding, arriving in zip(kept, incoming)
        )
    )


def rope_tables(places, head_width):
    freq = rope_base ** (-(jnp.arange(0, head_width, 2, dtype=jnp.float32) / head_width))
    angle = places.astype(jnp.float32)[:, None, None] * freq[None, None, :]
    return (jnp.cos(angle), jnp.sin(angle))


def turn(part, cosine, sine):
    half = part.shape[-1] // 2
    first_half = part[..., :half]
    second_half = part[..., half:]
    return jnp.concatenate(
        [first_half * cosine - second_half * sine, second_half * cosine + first_half * sine],
        axis=-1,
    )


def turn_back(grad, cosine, sine):
    half = grad.shape[-1] // 2
    first_half = grad[..., :half]
    second_half = grad[..., half:]
    return jnp.concatenate(
        [first_half * cosine + second_half * sine, second_half * cosine - first_half * sine],
        axis=-1,
    )


def norm_forward(value, gain):
    center = value - jnp.mean(value, axis=-1, keepdims=True)
    inverse = lax.rsqrt(jnp.mean(center * center, axis=-1, keepdims=True) + epsilon)
    normed = center * inverse
    return (normed * gain, normed, inverse)


def norm_backward(grad, gain, normed, inverse):
    scaled = grad * gain
    back = inverse * (
        scaled
        - jnp.mean(scaled, axis=-1, keepdims=True)
        - normed * jnp.mean(scaled * normed, axis=-1, keepdims=True)
    )
    return (back, jnp.sum(grad * normed, axis=0))


def geglu(first_part, second_part):
    return jax.nn.gelu(first_part, approximate=False) * second_part


def attend(by_head, segment):
    capacity, head_count, triple_width = by_head.shape
    head_width = triple_width // 3
    block_rows = min(512, capacity)
    block_count = capacity // block_rows
    keys = by_head[:, :, head_width : 2 * head_width]
    values = by_head[:, :, 2 * head_width :]
    factor = 1.0 / math.sqrt(head_width)

    def one_block(position):
        first = position * block_rows
        query = lax.dynamic_slice_in_dim(by_head, first, block_rows, 0)[:, :, :head_width]
        query_seg = lax.dynamic_slice_in_dim(segment, first, block_rows, 0)
        scores = (
            jnp.einsum("qhd,khd->hqk", query, keys, preferred_element_type=jnp.float32) * factor
        )
        same_seq = (query_seg[:, None] == segment[None, :])[None]
        scores = jnp.where(same_seq, scores, -1e30)
        top_score = jnp.max(scores, axis=-1, keepdims=True)
        raised = jnp.exp(scores - top_score)
        denominator = jnp.sum(raised, axis=-1, keepdims=True)
        probs = (raised / denominator).astype(jnp.bfloat16)
        attended = jnp.einsum(
            "hqk,khd->qhd", probs, values, preferred_element_type=jnp.float32
        ).astype(jnp.bfloat16)
        return (attended, (top_score + jnp.log(denominator))[..., 0])

    attended, log_totals = lax.map(one_block, jnp.arange(block_count, dtype=jnp.int32))
    return (attended.reshape(capacity, head_count, head_width), log_totals)


def attend_back(by_head, grad_out, log_totals, segment):
    capacity, head_count, triple_width = by_head.shape
    head_width = triple_width // 3
    block_rows = min(512, capacity)
    block_count = capacity // block_rows
    keys = by_head[:, :, head_width : 2 * head_width]
    values = by_head[:, :, 2 * head_width :]
    factor = 1.0 / math.sqrt(head_width)

    def one_block(sums, position):
        key_grads, value_grads = sums
        first = position * block_rows
        query = lax.dynamic_slice_in_dim(by_head, first, block_rows, 0)[:, :, :head_width]
        query_seg = lax.dynamic_slice_in_dim(segment, first, block_rows, 0)
        grad_rows = lax.dynamic_slice_in_dim(grad_out, first, block_rows, 0)
        scores = (
            jnp.einsum("qhd,khd->hqk", query, keys, preferred_element_type=jnp.float32) * factor
        )
        same_seq = (query_seg[:, None] == segment[None, :])[None]
        probs = jnp.where(same_seq, jnp.exp(scores - log_totals[position][:, :, None]), 0.0)
        grad_probs = jnp.einsum(
            "qhd,khd->hqk", grad_rows, values, preferred_element_type=jnp.float32
        )
        value_grads = value_grads + jnp.einsum(
            "hqk,qhd->khd",
            probs.astype(jnp.bfloat16),
            grad_rows,
            preferred_element_type=jnp.float32,
        )
        centered = jnp.sum(probs * grad_probs, axis=-1, keepdims=True)
        grad_scores = (probs * (grad_probs - centered)).astype(jnp.bfloat16)
        query_grads = (
            jnp.einsum("hqk,khd->qhd", grad_scores, keys, preferred_element_type=jnp.float32)
            * factor
        )
        key_grads = (
            key_grads
            + jnp.einsum("hqk,qhd->khd", grad_scores, query, preferred_element_type=jnp.float32)
            * factor
        )
        return ((key_grads, value_grads), query_grads)

    empty = jnp.zeros((capacity, head_count, head_width), jnp.float32)
    (key_grads, value_grads), query_grads = lax.scan(
        one_block, (empty, empty), jnp.arange(block_count, dtype=jnp.int32)
    )
    return (query_grads.reshape(capacity, head_count, head_width), key_grads, value_grads)


def local(
    tokens,
    gain_attn,
    w_qkv,
    w_out,
    gain_mlp,
    w_in,
    w_down,
    cotangent,
    seq_lengths,
    seq_offsets,
    deal,
):
    group_index = lax.axis_index("dp")
    row_index = lax.axis_index("row")
    row_count = CAP // lax.axis_size("row")
    source, places, segment = slot_table(seq_lengths, seq_offsets, deal, group_index)
    blank = jnp.zeros((CAP, tokens.shape[1]), jnp.bfloat16)
    group_in, group_grad = take_rows(
        (blank, blank),
        (
            lax.all_gather(tokens, "dp", axis=0, tiled=True),
            lax.all_gather(cotangent, "dp", axis=0, tiled=True),
        ),
        source,
    )
    w_query, w_proj, w_gate, w_lower = (
        lax.all_gather(w_qkv.astype(jnp.bfloat16), "row", axis=0, tiled=True),
        lax.all_gather(w_out.astype(jnp.bfloat16), "row", axis=1, tiled=True),
        lax.all_gather(w_in.astype(jnp.bfloat16), "row", axis=0, tiled=True),
        lax.all_gather(w_down.astype(jnp.bfloat16), "row", axis=1, tiled=True),
    )
    rows_in, rows_grad = (
        lax.all_to_all(group_in, "row", split_axis=0, concat_axis=1, tiled=True),
        lax.all_to_all(group_grad, "row", split_axis=0, concat_axis=1, tiled=True),
    )
    head_width = w_query.shape[2] // 3
    my_places = lax.dynamic_slice_in_dim(places, row_index * row_count, row_count)
    cosine, sine = rope_tables(my_places, head_width)
    resid = rows_in.astype(jnp.float32)
    normed_one, unit_one, inverse_one = norm_forward(resid, gain_attn)
    normed_one = normed_one.astype(jnp.bfloat16)
    triples = jnp.einsum("td,dhe->the", normed_one, w_query, preferred_element_type=jnp.float32)
    turned = jnp.concatenate(
        [
            turn(triples[..., :head_width], cosine, sine),
            turn(triples[..., head_width : 2 * head_width], cosine, sine),
            triples[..., 2 * head_width :],
        ],
        axis=-1,
    ).astype(jnp.bfloat16)
    by_head = lax.all_to_all(turned, "row", split_axis=1, concat_axis=0, tiled=True)
    attended, log_totals = attend(by_head, segment)
    attn_rows = lax.all_to_all(attended, "row", split_axis=0, concat_axis=1, tiled=True)
    attn_flat = attn_rows.reshape(row_count, -1)
    mixed = resid + lax.psum(jnp.dot(attn_flat, w_proj, preferred_element_type=jnp.float32), "col")
    normed_two, unit_two, inverse_two = norm_forward(mixed, gain_mlp)
    normed_two = normed_two.astype(jnp.bfloat16)
    both = jnp.einsum("td,dgf->tgf", normed_two, w_gate, preferred_element_type=jnp.float32)
    hidden_f32, geglu_back = jax.vjp(geglu, both[:, 0], both[:, 1])
    hidden = hidden_f32.astype(jnp.bfloat16)
    output_rows = (
        mixed
        + lax.psum(
            jnp.dot(hidden, w_lower, preferred_element_type=jnp.float32).astype(jnp.bfloat16), "col"
        ).astype(jnp.float32)
    ).astype(jnp.bfloat16)
    grad_hidden = jnp.einsum("td,fd->tf", rows_grad, w_lower, preferred_element_type=jnp.float32)
    lower_grad = jnp.einsum("tf,td->fd", hidden, rows_grad, preferred_element_type=jnp.float32)
    grad_first, grad_second = geglu_back(grad_hidden)
    grad_both = jnp.stack([grad_first, grad_second], axis=1).astype(jnp.bfloat16)
    gate_grad = jnp.einsum("td,tgf->dgf", normed_two, grad_both, preferred_element_type=jnp.float32)
    grad_normed_two = lax.psum(
        jnp.einsum("tgf,dgf->td", grad_both, w_gate, preferred_element_type=jnp.float32), "col"
    )
    back_two, gain_mlp_part = norm_backward(grad_normed_two, gain_mlp, unit_two, inverse_two)
    grad_mixed = rows_grad.astype(jnp.float32) + back_two
    grad_mixed_low = grad_mixed.astype(jnp.bfloat16)
    proj_grad = jnp.einsum(
        "te,td->ed", attn_flat, grad_mixed_low, preferred_element_type=jnp.float32
    )
    grad_attn = jnp.einsum(
        "td,ed->te", grad_mixed_low, w_proj, preferred_element_type=jnp.float32
    ).astype(jnp.bfloat16)
    grad_by_head = lax.all_to_all(
        grad_attn.reshape(attn_rows.shape), "row", split_axis=1, concat_axis=0, tiled=True
    )
    query_grads, key_grads, value_grads = attend_back(by_head, grad_by_head, log_totals, segment)
    group_cos, group_sin = rope_tables(places, head_width)
    grad_triples = jnp.concatenate(
        [
            turn_back(query_grads, group_cos, group_sin),
            turn_back(key_grads, group_cos, group_sin),
            value_grads,
        ],
        axis=-1,
    ).astype(jnp.bfloat16)
    grad_rows_triples = lax.all_to_all(grad_triples, "row", split_axis=0, concat_axis=1, tiled=True)
    query_weight_grad = jnp.einsum(
        "td,the->dhe", normed_one, grad_rows_triples, preferred_element_type=jnp.float32
    )
    grad_normed_one = lax.psum(
        jnp.einsum(
            "the,dhe->td", grad_rows_triples, w_query, preferred_element_type=jnp.float32
        ).astype(jnp.bfloat16),
        "col",
    ).astype(jnp.float32)
    back_one, gain_attn_part = norm_backward(grad_normed_one, gain_attn, unit_one, inverse_one)
    input_rows_grad = (grad_mixed + back_one).astype(jnp.bfloat16)
    gain_attn_grad, w_qkv_grad, w_out_grad, gain_mlp_grad, w_in_grad, w_down_grad = (
        lax.psum_scatter(gain_attn_part, ("dp", "row"), scatter_dimension=0, tiled=True),
        lax.psum_scatter(query_weight_grad, ("dp", "row"), scatter_dimension=0, tiled=True),
        lax.psum_scatter(proj_grad, ("dp", "row"), scatter_dimension=1, tiled=True),
        lax.psum_scatter(gain_mlp_part, ("dp", "row"), scatter_dimension=0, tiled=True),
        lax.psum_scatter(gate_grad, ("dp", "row"), scatter_dimension=0, tiled=True),
        lax.psum_scatter(lower_grad, ("dp", "row"), scatter_dimension=1, tiled=True),
    )
    width_out, width_grad = (
        lax.all_to_all(output_rows, "row", split_axis=1, concat_axis=0, tiled=True),
        lax.all_to_all(input_rows_grad, "row", split_axis=1, concat_axis=0, tiled=True),
    )
    target = home_slots(seq_lengths, seq_offsets, deal, group_index, tokens.shape[0])
    blank_out = jnp.zeros(tokens.shape, jnp.bfloat16)
    layer_out, tokens_grad = take_rows(
        (blank_out, blank_out),
        (
            lax.all_gather(width_out, "dp", axis=0, tiled=True),
            lax.all_gather(width_grad, "dp", axis=0, tiled=True),
        ),
        target,
    )
    return (
        layer_out,
        tokens_grad,
        gain_attn_grad,
        w_qkv_grad,
        w_out_grad,
        gain_mlp_grad,
        w_in_grad,
        w_down_grad,
    )


def solution(mesh):
    return jax.shard_map(
        local,
        mesh=mesh,
        in_specs=(
            P("dp", "row"),
            P(),
            P("row", "col", None),
            P("col", "row"),
            P(),
            P("row", None, "col"),
            P("col", "row"),
            P("dp", "row"),
            P(),
            P(),
            P(),
        ),
        out_specs=(
            P("dp", "row"),
            P("dp", "row"),
            P(("dp", "row")),
            P(("dp", "row"), "col", None),
            P("col", ("dp", "row")),
            P(("dp", "row")),
            P(("dp", "row"), None, "col"),
            P("col", ("dp", "row")),
        ),
        check_vma=False,
    )
```

profile of v0, /device:TPU:0, one launch (start us, length us, event | category | flops | bytes accessed | tf_op | source)
XLA Modules:
  0.0 1970.3 jit_solution(4929160542916677543)
XLA Ops:
  12.8 176.2 %all-gather.21.cloned.1.call-done = bf16[12288,512]{1,0:T(8,128)(2,1)} async-done(((bf16[1536,512]{1,0:T(8,128)(2,1)}), bf16[12288,512]{1,0:T(8,128)(2,1)}) %all-gather.21.cloned.1.call-update) | async-done | bytes 12582928 | tf_op jit(solution)/shard_map/all_gather | solution.py:215
  189.0 11.1 gather_fusion.2
  200.1 165.4 %all-gather.9.cloned.1.call-done = bf16[12288,512]{1,0:T(8,128)(2,1)} async-done(((bf16[1536,512]{1,0:T(8,128)(2,1)}), bf16[12288,512]{1,0:T(8,128)(2,1)}) %all-gather.9.cloned.1.call-update) | async-done | bytes 12582928 | tf_op jit(solution)/shard_map/all_gather | solution.py:214
  365.5 11.1 gather_fusion
  383.7 35.8 %all-to-all-done = bf16[2,768,512]{2,1,0:T(8,128)(2,1)S(1)} async-done(((bf16[2,768,512]{2,1,0:T(8,128)(2,1)}), bf16[2,768,512]{2,1,0:T(8,128)(2,1)S(1)}, u32[]{:S(2)}, u32[]{:S(2)}) %all-to-all-start) | async-done | bytes 1572896 | tf_op jit(solution)/shard_map/all_to_all | solution.py:226
  429.5 4.7 fusion.84
  448.1 32.3 %all-to-all-done.1 = bf16[768,8,192]{0,2,1:T(8,128)(2,1)S(1)} async-done(((bf16[768,8,192]{0,2,1:T(8,128)(2,1)}), bf16[768,8,192]{0,2,1:T(8,128)(2,1)S(1)}, u32[]{:S(2)}, u32[]{:S(2)}) %all-to-all-start.1) | async-done | bytes 2359328 | tf_op jit(solution)/shard_map/all_to_all | solution.py:244
  481.9 40.5 %while.27 = (s32[]{:T(128)}, bf16[3,512,4,64]{1,3,2,0:T(8,128)(2,1)S(1)}, f32[3,4,512]{2,1,0:T(4,128)S(1)}, s32[3]{0:T(128)S(1)}, s32[1536]{0:T(1024)S(1)}, /*in...) while((s32[]{:T(128)}, ...), condition=%wide.region_18.20_spmd, body=%wide.region_15.19_spmd.sunk | while | flops 843970560 | bytes 43069636 | solution.py:140
  490.8 4.6 fusion.190
  504.3 4.6 fusion.190
  517.8 4.6 fusion.190
  527.0 12.0 all_to_all.139
  542.1 5.0 copy.124
  557.0 20.1 %all_to_all.140 = bf16[2,768,512]{2,1,0:T(8,128)(2,1)S(1)} all-to-all(bf16[2,768,512]{2,1,0:T(8,128)(2,1)} %bitcast.261), channel_id=1, replica_groups=mesh['dp'=8,'row'=2,'col'=2] {'row'}, dimensions={0} | all-to-all | bytes 3145728 | tf_op jit(solution)/shard_map/all_to_all | solution.py:227
  578.4 6.5 fusion.144
  585.0 5.8 fusion.141
  593.4 55.1 %all-gather.15.cloned.1.call-done = bf16[1024,2,1312]{0,2,1:T(8,128)(2,1)} async-done(((bf16[512,2,1312]{0,2,1:T(8,128)(2,1)}), bf16[1024,2,1312]{0,2,1:T(8,128)(2,1)}) %all-gather.15.cloned.1.call-update) | async-done | bytes 5373968 | tf_op jit(solution)/shard_map/all_gather | solution.py:222
  648.6 7.7 fusion.138
  656.3 9.9 fusion.79
  669.5 9.0 fusion.80
  678.5 23.4 %all-reduce.10.cloned.1.call-done = f32[768,1024]{1,0:T(8,128)} async-done(((f32[768,1024]{1,0:T(8,128)}), f32[768,1024]{1,0:T(8,128)}) %all-reduce.10.cloned.1.call-update) | async-done | bytes 3145744 | tf_op jit(solution)/shard_map/psum | solution.py:265
  701.9 4.7 multiply_reduce_fusion.1
  718.0 10.0 all-to-all-done.5
  733.2 110.9 %while.28 = (s32[]{:T(128)}, f32[1536,4,64]{0,2,1:T(8,128)}, f32[1536,4,64]{0,2,1:T(8,128)}, f32[3,512,4,64]{1,0,3,2:T(4,128)}, s32[3]{0:T(128)S(1)}, /*index=5*...) while((s32[]{:T(128)}, f32[1536,4,64]{0,2,1:T(8,128)}, ...), condition=%wide.region_28.30_spmd.clone, body=%wide.region_26.29_spmd.clone.sunk | while | flops 2044459008 | bytes 139776368 | solution.py:187
  739.9 5.4 multiply_reduce_fusion.7
  758.4 11.1 dynamic_update_slice.20
  776.1 5.4 multiply_reduce_fusion.7
  795.7 11.1 dynamic_update_slice.20
  813.5 5.4 multiply_reduce_fusion.7
  833.1 11.1 dynamic_update_slice.20
  854.5 5.7 copy.115
  864.3 9.2 fusion.81
  873.6 26.5 %all-to-all-done.6 = bf16[1536,4,192]{2,1,0:T(4,128)(2,1)S(1)} async-done(((bf16[1536,4,192]{2,1,0:T(4,128)(2,1)}), bf16[1536,4,192]{2,1,0:T(4,128)(2,1)S(1)}, u32[]{:S(2)}, u32[]{:S(2)}) %all-to-all-start.6) | async-done | bytes 2359328 | tf_op jit(solution)/shard_map/all_to_all | solution.py:290
  903.8 6.4 bitcast_convert_fusion
  913.3 5.6 fusion.145
  920.6 13.0 fusion.71
  937.1 56.3 %all_to_all.141 = bf16[768,2,512]{2,0,1:T(8,128)(2,1)} all-to-all(bf16[768,2,512]{2,0,1:T(8,128)(2,1)S(1)} %bitcast.259), channel_id=1, replica_groups=mesh['dp'=8,'row'=2,'col'=2] {'row'}, dimensions={1} | all-to-all | bytes 3145728 | tf_op jit(solution)/shard_map/all_to_all | solution.py:311
  997.8 55.0 %all_to_all.142 = bf16[768,2,512]{2,0,1:T(8,128)(2,1)} all-to-all(bf16[768,2,512]{2,0,1:T(8,128)(2,1)S(1)} %bitcast.260), channel_id=1, replica_groups=mesh['dp'=8,'row'=2,'col'=2] {'row'}, dimensions={1} | all-to-all | bytes 3145728 | tf_op jit(solution)/shard_map/all_to_all | solution.py:312
  1056.5 16.5 fusion.76
  1075.7 46.4 %all-reduce.2 = (f32[1024]{0:T(1024)S(1)}, f32[1024]{0:T(1024)S(1)}) all-reduce(f32[1024]{0:T(1024)S(1)} %get-tuple-element.202, f32[1024]{0:T(1024)S(1)} %copy-done.39), channel_id=2, replica_groups=mesh['dp'=8,'row'=2,'col'=2] {'dp','row'}, use_global_device_ids=true, to_apply=%region_33.35.clone | all-reduce | flops 2048 | bytes 16384
  1123.3 26.9 %reduce-scatter.5.cloned.1.call-done = f32[64,8,192]{2,0,1:T(8,128)} async-done(((f32[1024,8,192]{2,0,1:T(8,128)}), f32[64,8,192]{2,0,1:T(8,128)}) %reduce-scatter.5.cloned.1.call-update) | async-done | bytes 393232 | tf_op jit(solution)/shard_map/reduce_scatter | solution.py:304
  1152.4 244.7 %reduce-scatter.9.cloned.1.call-done = f32[64,2,1312]{2,0,1:T(8,128)} async-done(((f32[1024,2,1312]{2,0,1:T(8,128)}), f32[64,2,1312]{2,0,1:T(8,128)}) %reduce-scatter.9.cloned.1.call-update) | async-done | bytes 671760 | tf_op jit(solution)/shard_map/reduce_scatter | solution.py:307
  1399.6 179.3 %all-gather.19.cloned.1.call-done = bf16[12288,512]{1,0:T(8,128)(2,1)} async-done(((bf16[1536,512]{1,0:T(8,128)(2,1)}), bf16[12288,512]{1,0:T(8,128)(2,1)}) %all-gather.19.cloned.1.call-update) | async-done | bytes 12582928 | tf_op jit(solution)/shard_map/all_gather | solution.py:319
  1579.0 11.1 gather_fusion.1
  1590.0 165.4 %all-gather.23.cloned.1.call-done = bf16[12288,512]{1,0:T(8,128)(2,1)} async-done(((bf16[1536,512]{1,0:T(8,128)(2,1)}), bf16[12288,512]{1,0:T(8,128)(2,1)}) %all-gather.23.cloned.1.call-update) | async-done | bytes 12582928 | tf_op jit(solution)/shard_map/all_gather | solution.py:320
  1755.5 11.1 gather_fusion.3
  1768.9 68.9 %reduce-scatter.7.cloned.1.call-done = f32[512,64]{0,1:T(8,128)} async-done(((f32[512,1024]{0,1:T(8,128)}), f32[512,64]{0,1:T(8,128)}) %reduce-scatter.7.cloned.1.call-update) | async-done | bytes 131088 | tf_op jit(solution)/shard_map/reduce_scatter | solution.py:305
  1837.8 125.6 %reduce-scatter.11.cloned.1.call-done = f32[1312,64]{0,1:T(8,128)} async-done(((f32[1312,1024]{0,1:T(8,128)}), f32[1312,64]{0,1:T(8,128)}) %reduce-scatter.11.cloned.1.call-update) | async-done | bytes 335888 | tf_op jit(solution)/shard_map/reduce_scatter | solution.py:308
  (287 shorter events, 201.8 us)
Async XLA Ops:
  7.2 181.9 %all-gather.21.cloned.1.call-start = ((), (), s32[]{:S(2)}) async-start(), calls=%async_computation.19 | async-start | bytes 14155776 | tf_op jit(solution)/shard_map/all_gather | solution.py:215
  7.9 357.6 %all-gather.9.cloned.1.call-start = ((), (), s32[]{:S(2)}) async-start(), calls=%async_computation.12 | async-start | bytes 14155776 | tf_op jit(solution)/shard_map/all_gather | solution.py:214
  8.7 3.5 copy-start.46
  8.7 3.5 copy-start.40
  8.7 3.5 copy-start.44
  8.7 420.8 %all-gather.11.cloned.1.call-start = ((), (), s32[]{:S(2)}) async-start(), calls=%async_computation.13 | async-start | bytes 4718592 | tf_op jit(solution)/shard_map/all_gather | solution.py:220
  378.9 40.6 %all-to-all-start = ((bf16[2,768,512]{2,1,0:T(8,128)(2,1)}), bf16[2,768,512]{2,1,0:T(8,128)(2,1)S(1)}, u32[]{:S(2)}, u32[]{:S(2)}) async-start(bf16[2,768,512]{2,1,0:T(8,128)(2,1)} %bitcast.262), calls=%async_computation | async-start | bytes 3145728 | tf_op jit(solution)/shard_map/all_to_all | solution.py:226
  424.7 9.5 copy-start.4
  424.7 4.8 copy-start.34
  427.6 6.6 copy-start.26
  429.5 4.7 copy-start.30
  438.8 41.6 %all-to-all-start.1 = ((bf16[768,8,192]{0,2,1:T(8,128)(2,1)}), bf16[768,8,192]{0,2,1:T(8,128)(2,1)S(1)}, u32[]{:S(2)}, u32[]{:S(2)}) async-start(bf16[768,8,192]{0,2,1:T(8,128)(2,1)} %fusion.89), calls=%async_computation.1 | async-start | bytes 4718592 | tf_op jit(solution)/shard_map/all_to_all | solution.py:244
  442.6 105.7 %all-gather.13.cloned.1.call-start = ((), (), s32[]{:S(2)}) async-start(), calls=%async_computation.14 | async-start | bytes 1572864 | tf_op jit(solution)/shard_map/all_gather | solution.py:221
  444.9 133.5 %all-gather.17.cloned.1.call-start = ((), (), s32[]{:S(2)}) async-start(), calls=%async_computation.17 | async-start | bytes 4030464 | tf_op jit(solution)/shard_map/all_gather | solution.py:223
  448.0 136.9 %all-reduce.8.cloned.1.call-start = ((), (), s32[]{:S(2)}) async-start(), calls=%async_computation.15 | async-start | bytes 6291456 | tf_op jit(solution)/shard_map/psum | solution.py:248
  548.3 4.2 copy-start.16
  552.5 96.1 %all-gather.15.cloned.1.call-start = ((), (), s32[]{:S(2)}) async-start(), calls=%async_computation.16 | async-start | bytes 8060928 | tf_op jit(solution)/shard_map/all_gather | solution.py:222
  557.0 144.9 %all-reduce.10.cloned.1.call-start = ((), (), s32[]{:S(2)}) async-start(), calls=%async_computation.20 | async-start | bytes 6291456 | tf_op jit(solution)/shard_map/psum | solution.py:265
  590.8 57.8 %copy-start.37 = (f32[1024]{0:T(1024)S(1)}, f32[1024]{0:T(1024)}, u32[]{:S(2)}) copy-start(f32[1024]{0:T(1024)} %param.21) | copy-start | bytes 12292
  590.8 115.9 %copy-start.28 = (f32[768]{0:T(1024)}, f32[768]{0:T(1024)S(1)}, u32[]{:S(2)}) copy-start(f32[768]{0:T(1024)S(1)} %broadcast_multiply_fusion.4) | copy-start | bytes 9220
  593.4 113.2 %copy-start.32 = (f32[768]{0:T(1024)}, f32[768]{0:T(1024)S(1)}, u32[]{:S(2)}) copy-start(f32[768]{0:T(1024)S(1)} %add_rsqrt_fusion) | copy-start | bytes 9220
  648.6 7.7 copy-start.14
  656.3 9.9 copy-start.12
  701.9 4.7 copy-start.15
  701.9 4.8 copy-start.17
  706.7 4.3 copy-start.25
  711.0 5.5 copy-start.36
  711.0 5.5 copy-start.43
  713.0 15.0 all-to-all-start.5
  733.2 3.9 copy-start.1
  754.4 15.1 copy-start.2
  769.5 3.9 copy-start.1
  785.2 4.0 copy-start
  791.2 15.6 copy-start.2
  806.8 3.9 copy-start.1
  822.6 4.0 copy-start
  828.6 15.6 copy-start.2
  848.1 5.5 copy-start.3
  860.2 39.9 %all-to-all-start.6 = ((bf16[1536,4,192]{2,1,0:T(4,128)(2,1)}), bf16[1536,4,192]{2,1,0:T(4,128)(2,1)S(1)}, u32[]{:S(2)}, u32[]{:S(2)}) async-start(bf16[1536,4,192]{2,1,0:T(4,128)(2,1)} %copy.115), calls=%async_computation.6 | async-start | bytes 6291456 | tf_op jit(solution)/shard_map/all_to_all | solution.py:290
  864.1 69.9 %all-reduce.12.cloned.1.call-start = ((), (), s32[]{:S(2)}) async-start(), calls=%async_computation.26 | async-start | bytes 6291456 | tf_op jit(solution)/shard_map/psum | solution.py:256
  910.2 240.0 %reduce-scatter.5.cloned.1.call-start = ((), (), s32[]{:S(2)}) async-start(), calls=%async_computation.22 | async-start | bytes 8912896 | tf_op jit(solution)/shard_map/reduce_scatter | solution.py:304
  918.9 478.2 %reduce-scatter.9.cloned.1.call-start = ((), (), s32[]{:S(2)}) async-start(), calls=%async_computation.24 | async-start | bytes 12255232 | tf_op jit(solution)/shard_map/reduce_scatter | solution.py:307
  933.6 645.3 %all-gather.19.cloned.1.call-start = ((), (), s32[]{:S(2)}) async-start(), calls=%async_computation.18 | async-start | bytes 14155776 | tf_op jit(solution)/shard_map/all_gather | solution.py:319
  937.1 56.4 %copy-start.5 = (f32[768,1024]{1,0:T(8,128)S(1)}, f32[768,1024]{1,0:T(8,128)}, u32[]{:S(2)}) copy-start(f32[768,1024]{1,0:T(8,128)} %copy-done.4) | copy-start | bytes 9437188
  993.4 762.1 %all-gather.23.cloned.1.call-start = ((), (), s32[]{:S(2)}) async-start(), calls=%async_computation.21 | async-start | bytes 14155776 | tf_op jit(solution)/shard_map/all_gather | solution.py:320
  997.8 55.1 %copy-start.10 = (f32[768,1024]{1,0:T(8,128)S(1)}, f32[768,1024]{1,0:T(8,128)}, u32[]{:S(2)}) copy-start(f32[768,1024]{1,0:T(8,128)} %copy-done.8) | copy-start | bytes 9437188
  1052.8 784.9 %reduce-scatter.7.cloned.1.call-start = ((), (), s32[]{:S(2)}) async-start(), calls=%async_computation.23 | async-start | bytes 2228224 | tf_op jit(solution)/shard_map/reduce_scatter | solution.py:305
  1056.4 906.9 %reduce-scatter.11.cloned.1.call-start = ((), (), s32[]{:S(2)}) async-start(), calls=%async_computation.25 | async-start | bytes 6127616 | tf_op jit(solution)/shard_map/reduce_scatter | solution.py:308
  (26 other events, 48.1 us)
Sparse Core Ops, SparseCore 0:
  10.2 178.8 all-gather.20
  191.2 174.2 all-gather.8
  367.1 59.9 all-gather.10
  445.2 31.5 all-gather.12
  478.2 39.7 all-gather.16
  552.6 23.1 all-reduce.7
  577.3 71.1 all-gather.14
  678.6 23.2 all-reduce.9
  910.3 23.6 all-reduce.11
  936.2 214.0 reduce-scatter.4
  1152.5 244.5 reduce-scatter.8
  1399.2 179.7 all-gather.18
  1581.2 174.2 all-gather.22
  1758.2 79.5 reduce-scatter.6
  1840.5 122.7 reduce-scatter.10
where the time goes:
time: 1980 us; the launch traced here: 1970 us
  waiting for transfers between devices  1340 us (68%)
  blocking collectives  190 us (10%)
  matrix products  166 us (8%)
  local copies, waits for them, and re-layouts  138 us (7%)
  other arithmetic  97.8 us (5%)
    reduce_scatter x1, waiting for transfers between devices, local(): lax.psum_scatter(gate_grad, ('dp', 'row'), scatter_dimension=0, tiled=True)  245 us
    all_gather x1, waiting for transfers between devices, local(): lax.all_gather(width_out, 'dp', axis=0, tiled=True)  179 us
    all_gather x1, waiting for transfers between devices, local(): lax.all_gather(cotangent, 'dp', axis=0, tiled=True)  176 us
    all_gather x1, waiting for transfers between devices, local(): lax.all_gather(width_grad, 'dp', axis=0, tiled=True)  165 us
    all_gather x1, waiting for transfers between devices, local(): lax.all_gather(tokens, 'dp', axis=0, tiled=True)  165 us
    reduce_scatter x1, waiting for transfers between devices, local(): lax.psum_scatter(lower_grad, ('dp', 'row'), scatter_dimension=1, tiled=True)  126 us
    reduce_scatter x1, waiting for transfers between devices, local(): lax.psum_scatter(proj_grad, ('dp', 'row'), scatter_dimension=1, tiled=True)  68.9 us
    all_to_all x1, blocking collectives, local(): lax.all_to_all(output_rows, 'row', split_axis=1, concat_axis=0, tiled=True)  56.3 us
  transfers between devices with their start and end apart: 19, of which 15 were waited for; matrix products, arithmetic and copies ran while one was open for 11% of the time, Pallas kernels for 0%

commit v1 on v0

--- a/solution.py
+++ b/solution.py
@@ -8,6 +8,19 @@
 CAP = 1536
 epsilon = 1e-05
 rope_base = 160000.0
+
+
+def gather_around(array, axis, dim):
+    ways = lax.axis_size(axis)
+    up = [(d, (d + 1) % ways) for d in range(ways)]
+    down = [(d, (d - 1) % ways) for d in range(ways)]
+    earlier, later = ([array], [array])
+    for _ in range(ways // 2):
+        earlier.append(lax.ppermute(earlier[-1], axis, up))
+    for _ in range((ways - 1) // 2):
+        later.append(lax.ppermute(later[-1], axis, down))
+    line = jnp.concatenate([*earlier[::-1], *later[1:]], axis=dim)
+    return jnp.roll(line, (lax.axis_index(axis) - ways // 2) * array.shape[dim], axis=dim)
 
 
 def slot_table(seq_lengths, seq_offsets, deal, group_index):
@@ -315,10 +328,7 @@
     blank_out = jnp.zeros(tokens.shape, jnp.bfloat16)
     layer_out, tokens_grad = take_rows(
         (blank_out, blank_out),
-        (
-            lax.all_gather(width_out, "dp", axis=0, tiled=True),
-            lax.all_gather(width_grad, "dp", axis=0, tiled=True),
-        ),
+        (gather_around(width_out, "dp", 0), lax.all_gather(width_grad, "dp", axis=0, tiled=True)),
         target,
     )
     return (

time: 1980 us -> 1840 us (0.929)
  waiting for transfers between devices: 1340 us -> 1060 us
  blocking collectives: 190 us -> 283 us
  starting transfers between devices: 16.1 us -> 39.4 us
  local copies, waits for them, and re-layouts: 138 us -> 158 us
    ppermute x0 -> x7, waiting for transfers between devices: none -> 256 us  [the longest x4 158 us: gather_around(): earlier.append(lax.ppermute(earlier[-1], axis, up))]
    reduce_scatter x1, waiting for transfers between devices: 245 us -> 0.01 us  [local(): lax.psum_scatter(gate_grad, ('dp', 'row'), scatter_dimension=0, tiled=True)]
    all_gather x1 -> x0, waiting for transfers between devices: 179 us -> none  [local(): lax.all_gather(width_out, 'dp', axis=0, tiled=True)]
    unnamed x1, blocking collectives: 46.4 us -> 137 us
    all_gather x1, waiting for transfers between devices: 165 us -> 82.4 us  [local(): lax.all_gather(width_grad, 'dp', axis=0, tiled=True)]
    reduce_scatter x1, waiting for transfers between devices: 26.9 us -> 0.02 us  [local(): lax.psum_scatter(query_weight_grad, ('dp', 'row'), scatter_dimension=0, t...]
    ppermute x0 -> x7, starting transfers between devices: none -> 23.3 us  [the longest x3 14.8 us: gather_around(): later.append(lax.ppermute(later[-1], axis, down))]
  transfers between devices with their start and end apart: 19 -> 25, of which waited for: 15 -> 16; matrix products, arithmetic and copies ran while one was open for 11% -> 13% of each run, Pallas kernels for 0% -> 0%
where the time goes in v1:
time: 1840 us; the launch traced here: 1830 us
  waiting for transfers between devices  1060 us (58%)
  blocking collectives  283 us (15%)
  matrix products  167 us (9%)
  local copies, waits for them, and re-layouts  158 us (9%)
  other arithmetic  98.1 us (5%)
  starting transfers between devices  39.4 us (2%)
    all_gather x1, waiting for transfers between devices, local(): lax.all_gather(cotangent, 'dp', axis=0, tiled=True)  176 us
    all_gather x1, waiting for transfers between devices, local(): lax.all_gather(tokens, 'dp', axis=0, tiled=True)  165 us
    ppermute x4, waiting for transfers between devices, gather_around(): earlier.append(lax.ppermute(earlier[-1], axis, up))  158 us
    unnamed x1, blocking collectives  137 us
    reduce_scatter x1, waiting for transfers between devices, local(): lax.psum_scatter(lower_grad, ('dp', 'row'), scatter_dimension=1, tiled=True)  125 us
    ppermute x3, waiting for transfers between devices, gather_around(): later.append(lax.ppermute(later[-1], axis, down))  98.2 us
    all_gather x1, waiting for transfers between devices, local(): lax.all_gather(width_grad, 'dp', axis=0, tiled=True)  82.4 us
    reduce_scatter x1, waiting for transfers between devices, local(): lax.psum_scatter(proj_grad, ('dp', 'row'), scatter_dimension=1, tiled=True)  69.1 us
  transfers between devices with their start and end apart: 25, of which 16 were waited for; matrix products, arithmetic and copies ran while one was open for 13% of the time, Pallas kernels for 0%

profile of v1, /device:TPU:0, one launch (start us, length us, event | category | flops | bytes accessed | tf_op | source)
XLA Modules:
  0.0 1830.7 jit_solution(3743099029709377085)
XLA Ops:
  12.8 176.2 %all-gather.18.cloned.1.call-done = bf16[12288,512]{1,0:T(8,128)(2,1)} async-done(((bf16[1536,512]{1,0:T(8,128)(2,1)}), bf16[12288,512]{1,0:T(8,128)(2,1)}) %all-gather.18.cloned.1.call-update) | async-done | bytes 12582928 | tf_op jit(solution)/shard_map/all_gather | solution.py:228
  189.0 11.1 gather_fusion.2
  200.1 165.4 %all-gather.8.cloned.1.call-done = bf16[12288,512]{1,0:T(8,128)(2,1)} async-done(((bf16[1536,512]{1,0:T(8,128)(2,1)}), bf16[12288,512]{1,0:T(8,128)(2,1)}) %all-gather.8.cloned.1.call-update) | async-done | bytes 12582928 | tf_op jit(solution)/shard_map/all_gather | solution.py:227
  365.5 11.1 gather_fusion
  383.7 35.8 %all-to-all-done = bf16[2,768,512]{2,1,0:T(8,128)(2,1)S(1)} async-done(((bf16[2,768,512]{2,1,0:T(8,128)(2,1)}), bf16[2,768,512]{2,1,0:T(8,128)(2,1)S(1)}, u32[]{:S(2)}, u32[]{:S(2)}) %all-to-all-start) | async-done | bytes 1572896 | tf_op jit(solution)/shard_map/all_to_all | solution.py:239
  448.2 32.2 %all-to-all-done.1 = bf16[768,8,192]{0,2,1:T(8,128)(2,1)S(1)} async-done(((bf16[768,8,192]{0,2,1:T(8,128)(2,1)}), bf16[768,8,192]{0,2,1:T(8,128)(2,1)S(1)}, u32[]{:S(2)}, u32[]{:S(2)}) %all-to-all-start.1) | async-done | bytes 2359328 | tf_op jit(solution)/shard_map/all_to_all | solution.py:257
  482.0 40.5 %while.27 = (s32[]{:T(128)}, bf16[3,512,4,64]{1,3,2,0:T(8,128)(2,1)S(1)}, f32[3,4,512]{2,1,0:T(4,128)S(1)}, s32[3]{0:T(128)S(1)}, s32[1536]{0:T(1024)S(1)}, /*in...) while((s32[]{:T(128)}, ...), condition=%wide.region_18.20_spmd, body=%wide.region_15.19_spmd.sunk | while | flops 843970560 | bytes 43069636 | solution.py:153
  527.1 12.0 all_to_all.139
  542.2 5.0 copy.124
  557.2 20.1 %all_to_all.140 = bf16[2,768,512]{2,1,0:T(8,128)(2,1)S(1)} all-to-all(bf16[2,768,512]{2,1,0:T(8,128)(2,1)} %bitcast.264), channel_id=1, replica_groups=mesh['dp'=8,'row'=2,'col'=2] {'row'}, dimensions={0} | all-to-all | bytes 3145728 | tf_op jit(solution)/shard_map/all_to_all | solution.py:240
  578.6 6.5 fusion.144
  585.1 5.8 fusion.141
  593.6 55.1 %all-gather.14.cloned.1.call-done = bf16[1024,2,1312]{0,2,1:T(8,128)(2,1)} async-done(((bf16[512,2,1312]{0,2,1:T(8,128)(2,1)}), bf16[1024,2,1312]{0,2,1:T(8,128)(2,1)}) %all-gather.14.cloned.1.call-update) | async-done | bytes 5373968 | tf_op jit(solution)/shard_map/all_gather | solution.py:235
  648.7 7.7 fusion.138
  656.5 9.9 fusion.79
  669.8 9.0 fusion.80
  678.8 23.4 %all-reduce.10.cloned.1.call-done = f32[768,1024]{1,0:T(8,128)} async-done(((f32[768,1024]{1,0:T(8,128)}), f32[768,1024]{1,0:T(8,128)}) %all-reduce.10.cloned.1.call-update) | async-done | bytes 3145744 | tf_op jit(solution)/shard_map/psum | solution.py:278
  718.7 10.0 all-to-all-done.5
  733.9 111.1 %while.28 = (s32[]{:T(128)}, f32[1536,4,64]{0,2,1:T(8,128)}, f32[1536,4,64]{0,2,1:T(8,128)}, f32[3,512,4,64]{1,0,3,2:T(4,128)}, s32[3]{0:T(128)S(1)}, /*index=5*...) while((s32[]{:T(128)}, f32[1536,4,64]{0,2,1:T(8,128)}, ...), condition=%wide.region_28.30_spmd.clone, body=%wide.region_26.29_spmd.clone.sunk | while | flops 2044459008 | bytes 139776368 | solution.py:200
  740.5 5.4 multiply_reduce_fusion.7
  759.1 11.1 dynamic_update_slice.20
  776.8 5.4 multiply_reduce_fusion.7
  796.5 11.1 dynamic_update_slice.20
  814.2 5.4 multiply_reduce_fusion.7
  833.9 11.1 dynamic_update_slice.20
  855.2 5.7 copy.115
  865.1 9.2 fusion.81
  874.3 26.5 %all-to-all-done.6 = bf16[1536,4,192]{2,1,0:T(4,128)(2,1)S(1)} async-done(((bf16[1536,4,192]{2,1,0:T(4,128)(2,1)}), bf16[1536,4,192]{2,1,0:T(4,128)(2,1)S(1)}, u32[]{:S(2)}, u32[]{:S(2)}) %all-to-all-start.6) | async-done | bytes 2359328 | tf_op jit(solution)/shard_map/all_to_all | solution.py:303
  904.5 6.5 bitcast_convert_fusion
  911.7 7.3 fusion.145
  920.5 13.3 fusion.71
  940.2 58.4 %all_to_all.141 = bf16[768,2,512]{2,0,1:T(8,128)(2,1)} all-to-all(bf16[768,2,512]{2,0,1:T(8,128)(2,1)S(1)} %bitcast.262), channel_id=1, replica_groups=mesh['dp'=8,'row'=2,'col'=2] {'row'}, dimensions={1} | all-to-all | bytes 3145728 | tf_op jit(solution)/shard_map/all_to_all | solution.py:325
  1001.3 55.2 %all_to_all.142 = bf16[768,2,512]{2,0,1:T(8,128)(2,1)S(1)} all-to-all(bf16[768,2,512]{2,0,1:T(8,128)(2,1)S(1)} %bitcast.263), channel_id=1, replica_groups=mesh['dp'=8,'row'=2,'col'=2] {'row'}, dimensions={1} | all-to-all | bytes 3145728 | tf_op jit(solution)/shard_map/all_to_all | solution.py:324
  1056.5 5.5 collective-permute-start
  1064.4 62.4 %collective-permute-done = bf16[1536,512]{1,0:T(8,128)(2,1)} collective-permute-done((bf16[1536,512]{1,0:T(8,128)(2,1)S(1)}, bf16[1536,512]{1,0:T(8,128)(2,1)}, u32[]{:S(2)}, u32[]{:S(2)}) %collective-permute-start) | collective-permute-done | bytes 1572896 | tf_op jit(solution)/shard_map/ppermute | solution.py:19
  1127.3 16.1 fusion.76
  1143.4 5.6 collective-permute-start.4
  1149.0 95.8 %collective-permute-done.1 = bf16[1536,512]{1,0:T(8,128)(2,1)} collective-permute-done((bf16[1536,512]{1,0:T(8,128)(2,1)}, bf16[1536,512]{1,0:T(8,128)(2,1)}, u32[]{:S(2)}, u32[]{:S(2)}) %collective-permute-start.1) | collective-permute-done | bytes 1572896 | tf_op jit(solution)/shard_map/ppermute | solution.py:19
  1247.4 70.4 %collective-permute-done.4 = bf16[1536,512]{1,0:T(8,128)(2,1)S(1)} collective-permute-done((bf16[1536,512]{1,0:T(8,128)(2,1)S(1)}, bf16[1536,512]{1,0:T(8,128)(2,1)S(1)}, u32[]{:S(2)}, u32[]{:S(2)}) %collective-permute-start.4) | collective-permute-done | bytes 1572896 | tf_op jit(solution)/shard_map/ppermute | solution.py:21
  1322.2 137.3 %all-reduce.2 = (f32[1024]{0:T(1024)S(1)}, f32[1024]{0:T(1024)S(1)}) all-reduce(f32[1024]{0:T(1024)S(1)} %get-tuple-element.202, f32[1024]{0:T(1024)S(1)} %copy-done.40), channel_id=2, replica_groups=mesh['dp'=8,'row'=2,'col'=2] {'dp','row'}, use_global_device_ids=true, to_apply=%region_33.35.clone | all-reduce | flops 2048 | bytes 16384
  1460.7 7.0 collective-permute-start.6
  1475.5 27.8 %collective-permute-done.6 = bf16[1536,512]{1,0:T(8,128)(2,1)S(1)} collective-permute-done((bf16[1536,512]{1,0:T(8,128)(2,1)}, bf16[1536,512]{1,0:T(8,128)(2,1)S(1)}, u32[]{:S(2)}, u32[]{:S(2)}) %collective-permute-start.6) | collective-permute-done | bytes 1572896 | tf_op jit(solution)/shard_map/ppermute | solution.py:21
  1511.7 6.5 constant_dynamic-slice_fusion
  1518.3 11.1 gather_fusion.1
  1534.1 82.4 %all-gather.20.cloned.1.call-done = bf16[12288,512]{1,0:T(8,128)(2,1)} async-done(((bf16[1536,512]{1,0:T(8,128)(2,1)}), bf16[12288,512]{1,0:T(8,128)(2,1)}) %all-gather.20.cloned.1.call-update) | async-done | bytes 12582928 | tf_op jit(solution)/shard_map/all_gather | solution.py:331
  1616.5 11.1 gather_fusion.3
  1629.9 69.1 %reduce-scatter.7.cloned.1.call-done = f32[512,64]{0,1:T(8,128)} async-done(((f32[512,1024]{0,1:T(8,128)}), f32[512,64]{0,1:T(8,128)}) %reduce-scatter.7.cloned.1.call-update) | async-done | bytes 131088 | tf_op jit(solution)/shard_map/reduce_scatter | solution.py:318
  1698.9 124.8 %reduce-scatter.11.cloned.1.call-done = f32[1312,64]{0,1:T(8,128)} async-done(((f32[1312,1024]{0,1:T(8,128)}), f32[1312,64]{0,1:T(8,128)}) %reduce-scatter.11.cloned.1.call-update) | async-done | bytes 335888 | tf_op jit(solution)/shard_map/reduce_scatter | solution.py:321
  (317 shorter events, 244.1 us)
Async XLA Ops:
  7.2 181.9 %all-gather.18.cloned.1.call-start = ((), (), s32[]{:S(2)}) async-start(), calls=%async_computation.18 | async-start | bytes 14155776 | tf_op jit(solution)/shard_map/all_gather | solution.py:228
  7.9 357.6 %all-gather.8.cloned.1.call-start = ((), (), s32[]{:S(2)}) async-start(), calls=%async_computation.12 | async-start | bytes 14155776 | tf_op jit(solution)/shard_map/all_gather | solution.py:227
  8.7 420.8 %all-gather.10.cloned.1.call-start = ((), (), s32[]{:S(2)}) async-start(), calls=%async_computation.13 | async-start | bytes 4718592 | tf_op jit(solution)/shard_map/all_gather | solution.py:233
  378.9 40.6 %all-to-all-start = ((bf16[2,768,512]{2,1,0:T(8,128)(2,1)}), bf16[2,768,512]{2,1,0:T(8,128)(2,1)S(1)}, u32[]{:S(2)}, u32[]{:S(2)}) async-start(bf16[2,768,512]{2,1,0:T(8,128)(2,1)} %bitcast.265), calls=%async_computation | async-start | bytes 3145728 | tf_op jit(solution)/shard_map/all_to_all | solution.py:239
  422.3 7.2 copy-start.35
  424.7 9.5 copy-start.4
  438.8 41.6 %all-to-all-start.1 = ((bf16[768,8,192]{0,2,1:T(8,128)(2,1)}), bf16[768,8,192]{0,2,1:T(8,128)(2,1)S(1)}, u32[]{:S(2)}, u32[]{:S(2)}) async-start(bf16[768,8,192]{0,2,1:T(8,128)(2,1)} %fusion.89), calls=%async_computation.1 | async-start | bytes 4718592 | tf_op jit(solution)/shard_map/all_to_all | solution.py:257
  442.6 105.8 %all-gather.12.cloned.1.call-start = ((), (), s32[]{:S(2)}) async-start(), calls=%async_computation.14 | async-start | bytes 1572864 | tf_op jit(solution)/shard_map/all_gather | solution.py:234
  445.0 133.6 %all-gather.16.cloned.1.call-start = ((), (), s32[]{:S(2)}) async-start(), calls=%async_computation.17 | async-start | bytes 4030464 | tf_op jit(solution)/shard_map/all_gather | solution.py:236
  448.1 137.0 %all-reduce.8.cloned.1.call-start = ((), (), s32[]{:S(2)}) async-start(), calls=%async_computation.15 | async-start | bytes 6291456 | tf_op jit(solution)/shard_map/psum | solution.py:261
  552.6 96.1 %all-gather.14.cloned.1.call-start = ((), (), s32[]{:S(2)}) async-start(), calls=%async_computation.16 | async-start | bytes 8060928 | tf_op jit(solution)/shard_map/all_gather | solution.py:235
  557.2 145.1 %all-reduce.10.cloned.1.call-start = ((), (), s32[]{:S(2)}) async-start(), calls=%async_computation.19 | async-start | bytes 6291456 | tf_op jit(solution)/shard_map/psum | solution.py:278
  585.1 63.6 %copy-start.38 = (f32[1024]{0:T(1024)S(1)}, f32[1024]{0:T(1024)}, u32[]{:S(2)}) copy-start(f32[1024]{0:T(1024)} %param.21) | copy-start | bytes 12292
  591.0 116.0 %copy-start.29 = (f32[768]{0:T(1024)}, f32[768]{0:T(1024)S(1)}, u32[]{:S(2)}) copy-start(f32[768]{0:T(1024)S(1)} %broadcast_multiply_fusion.4) | copy-start | bytes 9220
  593.6 113.3 %copy-start.33 = (f32[768]{0:T(1024)}, f32[768]{0:T(1024)S(1)}, u32[]{:S(2)}) copy-start(f32[768]{0:T(1024)S(1)} %add_rsqrt_fusion) | copy-start | bytes 9220
  648.7 7.7 copy-start.14
  656.5 9.9 copy-start.12
  713.6 15.0 all-to-all-start.5
  733.9 114.0 %copy-start.20 = (f32[1536,32]{0,1:T(8,128)S(1)}, f32[1536,32]{0,1:T(8,128)}, u32[]{:S(2)}) copy-start(f32[1536,32]{0,1:T(8,128)} %get-tuple-element.271) | copy-start | bytes 589828
  733.9 114.0 %copy-start.21 = (f32[1536,32]{0,1:T(8,128)S(1)}, f32[1536,32]{0,1:T(8,128)}, u32[]{:S(2)}) copy-start(f32[1536,32]{0,1:T(8,128)} %get-tuple-element.272) | copy-start | bytes 589828
  755.1 15.1 copy-start.2
  791.9 15.6 copy-start.2
  829.3 15.6 copy-start.2
  860.9 39.9 %all-to-all-start.6 = ((bf16[1536,4,192]{2,1,0:T(4,128)(2,1)}), bf16[1536,4,192]{2,1,0:T(4,128)(2,1)S(1)}, u32[]{:S(2)}, u32[]{:S(2)}) async-start(bf16[1536,4,192]{2,1,0:T(4,128)(2,1)} %copy.115), calls=%async_computation.6 | async-start | bytes 6291456 | tf_op jit(solution)/shard_map/all_to_all | solution.py:303
  864.9 70.0 %all-reduce.12.cloned.1.call-start = ((), (), s32[]{:S(2)}) async-start(), calls=%async_computation.25 | async-start | bytes 6291456 | tf_op jit(solution)/shard_map/psum | solution.py:269
  904.5 6.6 copy-start.28
  904.5 6.6 copy-start.32
  911.1 618.3 %reduce-scatter.5.cloned.1.call-start = ((), (), s32[]{:S(2)}) async-start(), calls=%async_computation.21 | async-start | bytes 8912896 | tf_op jit(solution)/shard_map/reduce_scatter | solution.py:317
  919.0 612.6 %reduce-scatter.9.cloned.1.call-start = ((), (), s32[]{:S(2)}) async-start(), calls=%async_computation.23 | async-start | bytes 12255232 | tf_op jit(solution)/shard_map/reduce_scatter | solution.py:320
  933.9 682.6 %all-gather.20.cloned.1.call-start = ((), (), s32[]{:S(2)}) async-start(), calls=%async_computation.20 | async-start | bytes 14155776 | tf_op jit(solution)/shard_map/all_gather | solution.py:331
  940.1 58.6 %copy-start.25 = (bf16[768,1024]{1,0:T(8,128)(2,1)S(1)}, bf16[768,1024]{1,0:T(8,128)(2,1)}, u32[]{:S(2)}) copy-start(bf16[768,1024]{1,0:T(8,128)(2,1)} %get-tuple-element.253) | copy-start | bytes 4718596
  998.6 700.3 %reduce-scatter.7.cloned.1.call-start = ((), (), s32[]{:S(2)}) async-start(), calls=%async_computation.22 | async-start | bytes 2228224 | tf_op jit(solution)/shard_map/reduce_scatter | solution.py:318
  1001.2 60.8 %copy-start.10 = (f32[768,1024]{1,0:T(8,128)S(1)}, f32[768,1024]{1,0:T(8,128)}, u32[]{:S(2)}) copy-start(f32[768,1024]{1,0:T(8,128)} %copy-done.8) | copy-start | bytes 9437188
  1001.2 60.8 %copy-start.17 = (bf16[768,2,4,64]{0,3,2,1:T(8,128)(2,1)S(1)}, bf16[768,2,4,64]{0,3,2,1:T(8,128)(2,1)}, u32[]{:S(2)}) copy-start(bf16[768,2,4,64]{0,3,2,1:T(8,128)(2,1)} %copy-done.16) | copy-start | bytes 2359300
  1056.5 70.8 %copy-start.18 = (bf16[2,96,8,512]{3,2,0,1:T(8,128)(2,1)S(1)}, bf16[2,96,8,512]{3,2,0,1:T(8,128)(2,1)}, u32[]{:S(2)}) copy-start(bf16[2,96,8,512]{3,2,0,1:T(8,128)(2,1)} %copy.142) | copy-start | bytes 4718596
  1056.5 70.3 %collective-permute-start = (bf16[1536,512]{1,0:T(8,128)(2,1)S(1)}, bf16[1536,512]{1,0:T(8,128)(2,1)}, u32[]{:S(2)}, u32[]{:S(2)}) collective-permute-start(bf16[1536,512]{1,0:T(8,128)(2,1)S(1)} %bitcast.241), channel_id=1, source_target_pairs={{0,4},{4,8},{8,12},{12,16},{16,20},{20,24},{24,28},{28,0},{1,5},{5... | collective-permute-start | bytes 4718600 | tf_op jit(solution)/shard_map/ppermute | solution.py:19
  1064.3 759.4 %reduce-scatter.11.cloned.1.call-start = ((), (), s32[]{:S(2)}) async-start(), calls=%async_computation.24 | async-start | bytes 6127616 | tf_op jit(solution)/shard_map/reduce_scatter | solution.py:321
  1126.8 118.0 %collective-permute-start.1 = (bf16[1536,512]{1,0:T(8,128)(2,1)}, bf16[1536,512]{1,0:T(8,128)(2,1)}, u32[]{:S(2)}, u32[]{:S(2)}) collective-permute-start(bf16[1536,512]{1,0:T(8,128)(2,1)} %collective-permute-done), channel_id=1, source_target_pairs={{0,4},{4,8},{8,12},{12,16},{16,20},{20,24},{24,28},{28,0},{1,5},{5... | collective-permute-start | bytes 4718600 | tf_op jit(solution)/shard_map/ppermute | solution.py:19
  1143.4 176.7 %copy-start.46 = (s32[16]{0:T(128)S(1)}, s32[16]{0:T(128)}, u32[]{:S(2)}) copy-start(s32[16]{0:T(128)} %param.25) | copy-start | bytes 196
  1143.4 176.7 %copy-start.48 = (s32[16]{0:T(128)S(1)}, s32[16]{0:T(128)}, u32[]{:S(2)}) copy-start(s32[16]{0:T(128)} %param.27) | copy-start | bytes 196
  1143.4 177.1 %copy-start.49 = (u32[32]{0:T(128)S(1)}, u32[32]{0:T(128)}, u32[]{:S(2)}) copy-start(u32[32]{0:T(128)} %constant.210) | copy-start | bytes 388
  1143.4 178.5 %copy-start.42 = (s32[16]{0:T(128)S(1)}, s32[16]{0:T(128)}, u32[]{:S(2)}) copy-start(s32[16]{0:T(128)} %param.26) | copy-start | bytes 196
  1143.4 178.8 %copy-start.40 = (f32[1024]{0:T(1024)S(1)}, f32[1024]{0:T(1024)}, u32[]{:S(2)}) copy-start(f32[1024]{0:T(1024)} %get-tuple-element.200) | copy-start | bytes 12292
  1143.4 174.4 %collective-permute-start.4 = (bf16[1536,512]{1,0:T(8,128)(2,1)S(1)}, bf16[1536,512]{1,0:T(8,128)(2,1)S(1)}, u32[]{:S(2)}, u32[]{:S(2)}) collective-permute-start(bf16[1536,512]{1,0:T(8,128)(2,1)S(1)} %bitcast.242), channel_id=1, source_target_pairs={{0,28},{4,0},{8,4},{12,8},{16,12},{20,16},{24,20},{28,24},{1,29},{... | collective-permute-start | bytes 4718600 | tf_op jit(solution)/shard_map/ppermute | solution.py:21
  1244.8 75.3 %collective-permute-start.2 = (bf16[1536,512]{1,0:T(8,128)(2,1)}, bf16[1536,512]{1,0:T(8,128)(2,1)}, u32[]{:S(2)}, u32[]{:S(2)}) collective-permute-start(bf16[1536,512]{1,0:T(8,128)(2,1)} %collective-permute-done.1), channel_id=1, source_target_pairs={{0,4},{4,8},{8,12},{12,16},{16,20},{20,24},{24,28},{28,0},{1,5},{5... | collective-permute-start | bytes 4718600 | tf_op jit(solution)/shard_map/ppermute | solution.py:19
  1317.9 142.8 %collective-permute-start.5 = (bf16[1536,512]{1,0:T(8,128)(2,1)S(1)}, bf16[1536,512]{1,0:T(8,128)(2,1)}, u32[]{:S(2)}, u32[]{:S(2)}) collective-permute-start(bf16[1536,512]{1,0:T(8,128)(2,1)S(1)} %collective-permute-done.4), channel_id=1, source_target_pairs={{0,28},{4,0},{8,4},{12,8},{16,12},{20,16},{24,20},{28,24},{1,29},{... | collective-permute-start | bytes 4718600 | tf_op jit(solution)/shard_map/ppermute | solution.py:21
  1320.0 147.6 %collective-permute-start.3 = (bf16[1536,512]{1,0:T(8,128)(2,1)}, bf16[1536,512]{1,0:T(8,128)(2,1)}, u32[]{:S(2)}, u32[]{:S(2)}) collective-permute-start(bf16[1536,512]{1,0:T(8,128)(2,1)} %collective-permute-done.2), channel_id=1, source_target_pairs={{0,4},{4,8},{8,12},{12,16},{16,20},{20,24},{24,28},{28,0},{1,5},{5... | collective-permute-start | bytes 4718600 | tf_op jit(solution)/shard_map/ppermute | solution.py:19
  1460.7 42.6 %collective-permute-start.6 = (bf16[1536,512]{1,0:T(8,128)(2,1)}, bf16[1536,512]{1,0:T(8,128)(2,1)S(1)}, u32[]{:S(2)}, u32[]{:S(2)}) collective-permute-start(bf16[1536,512]{1,0:T(8,128)(2,1)} %collective-permute-done.5), channel_id=1, source_target_pairs={{0,28},{4,0},{8,4},{12,8},{16,12},{20,16},{24,20},{28,24},{1,29},{... | collective-permute-start | bytes 4718600 | tf_op jit(solution)/shard_map/ppermute | solution.py:21
  (33 other events, 118.5 us)
Sparse Core Ops, SparseCore 0:
  10.2 178.8 all-gather.17
  191.2 174.2 all-gather.7
  367.1 59.9 all-gather.9
  445.2 31.5 all-gather.11
  478.2 39.7 all-gather.15
  552.7 23.1 all-reduce.7
  577.5 71.1 all-gather.13
  678.9 23.3 all-reduce.9
  911.2 23.6 all-reduce.11
  937.0 219.7 reduce-scatter.4
  1159.1 244.8 reduce-scatter.8
  1406.1 210.3 all-gather.19
  1619.3 79.5 reduce-scatter.6
  1701.7 122.0 reduce-scatter.10
